TPU v7x, 128 devices: a whole 4x4x4 slice. The times are simulated.
128 devices in a mesh: tm: 16 (over y, z), env: 8 (over x, core).
Axes of the slice: x: 4, y: 4, z: 4, core: 2. Of those that a mesh axis runs over, the one named last changes fastest.
Arguments:
- rewards: float32 [32768, 4096], P('tm', 'env'), may hold values from -0.16 to 0.16
- values: float32 [32768, 4096], P('tm', 'env'), may hold values from -6 to 6
- last_value: float32 [4096], P('env'), may hold values from -6 to 6
- done_steps: int32 [4096, 4], P('env'), may hold values from 0 to 32767
- horizon_offset: int32 [4096], P('env'), may hold values from 0 to 16383
- discount_rate: float32 [4096], P('env'), may hold values from 1.5258789e-06 to 0.03
- trace_rate: float32 [4096], P('env'), may hold values from 1.5258789e-06 to 0.03
Outputs:
- norm_advantages: float32 [4096, 32768], P(('env', 'tm'))
- norm_returns: float32 [4096, 32768], P(('env', 'tm'))
Inputs may be any that keep to these rules, and one draw needn't show every extreme that they name: `done_steps`: a repeated step in one environment's list is one termination.
All inputs are finite; a program needn't handle non-finite values.
Results may differ from a plain program's by a relative error of at most 0.0008.
Values sent between devices are 32-bit elements; how exact they have to be, the bound alone decides.
No kernel may reach another device: no remote copies, remote signals or barrier semaphores. Data moves between devices by JAX's collectives and lax.ppermute only.
A program may use at most 128 MiB of HBM per device.

v0:
```python
import jax
import jax.numpy as jnp
from jax import lax
from jax.sharding import Mesh
from jax.sharding import PartitionSpec as P

TM = ("tm_0", "tm_1")
ENV = ("env_0", "env_1")
TM_ENV = ("tm_0", "tm_1", "env_0", "env_1")
ENV_TM = ("env_0", "env_1", "tm_0", "tm_1")


def by_axis(value, axes):
    for axis in axes:
        value = lax.psum(value, axis)
    return value


def from_behind(block, axis, distance):
    devices = range(lax.axis_size(axis))
    route = [(i - distance, i) for i in devices if i - distance in devices]
    return lax.ppermute(block, axis, route)


def copy_for_each(value, axis):
    size = lax.axis_size(axis)
    return lax.all_to_all(
        jnp.broadcast_to(value[None], (size, *value.shape)), axis, 0, 0, tiled=True
    )


def all_in_one(value, axis):
    leaves = jax.tree.leaves(value)
    order = sorted(range(len(leaves)), key=lambda k: -leaves[k].size)
    width = (1, *leaves[order[0]].shape)[-1]
    lines = [
        jnp.pad(leaves[k].reshape(-1), (0, -leaves[k].size % width)).reshape(-1, width)
        for k in order
    ]
    both, at, found = (copy_for_each(jnp.concatenate(lines), axis), 0, {})
    for k, line in zip(order, lines):
        piece = both[:, at : at + len(line)].reshape(len(both), -1)
        found[k] = piece[:, : leaves[k].size].reshape(-1, *leaves[k].shape)
        at += len(line)
    numbers = iter(range(len(leaves)))
    return jax.tree.map(lambda _: found[next(numbers)], value)


def combined_pairwise(pieces, combine):
    while len(jax.tree.leaves(pieces)[0]) > 1:
        pieces = jax.vmap(combine)(
            *(jax.tree.map(lambda part: part[side::2], pieces) for side in (0, 1))
        )
    return jax.tree.map(lambda part: part[0], pieces)


def prefix(value, axis, combine, identity):
    size, here = (lax.axis_size(axis), lax.axis_index(axis))
    passed = jnp.arange(size) > here

    def kept(part, zero, own):
        part = jnp.where(
            passed.reshape(-1, *(1 for _ in own.shape)), part, jnp.asarray(zero, own.dtype)
        )
        return part[::-1]

    pieces = all_in_one(value, axis)
    return combined_pairwise(jax.tree.map(kept, pieces, identity, value), combine)


def episode_masks(moment_index, ends, offsets, horizon):
    finished = jnp.zeros_like(moment_index + offsets, dtype=bool)
    for column in ends:
        finished = finished | (moment_index == column)
    truncated = (moment_index + offsets) % horizon == horizon - 1
    living = 1.0 - finished.astype(jnp.float32)
    carried = living * (1.0 - truncated.astype(jnp.float32))
    return (living, carried)


def shift_later(field, distance, axis, filler):
    length = field.shape[axis]
    kept = lax.slice_in_dim(field, distance, length, 1, axis)
    shape = list(field.shape)
    shape[axis] = distance
    pad_block = jnp.full(tuple(shape), filler, field.dtype)
    return jnp.concatenate([kept, pad_block], axis=axis)


def suffix_scan(td_error, decay, axis):
    length = td_error.shape[axis]
    partial_value = td_error
    decayed = decay
    distance = 1
    while distance < length:
        later_partial = shift_later(partial_value, distance, axis, 0.0)
        later_decayed = shift_later(decayed, distance, axis, 1.0)
        partial_value = partial_value + decayed * later_partial
        decayed = decayed * later_decayed
        distance = distance * 2
    return (partial_value, decayed)


def compose_blocks(earlier, later):
    return (later[0] + later[1] * earlier[0], later[1] * earlier[1])


def statistics(advantages, returns):
    devices = lax.axis_size(TM) * lax.axis_size(ENV)
    samples = float(advantages.size * devices)
    sum_adv, sum_ret = (by_axis(jnp.sum(advantages), TM_ENV), by_axis(jnp.sum(returns), TM_ENV))
    mean_adv = sum_adv / samples
    mean_ret = sum_ret / samples
    dev_adv = advantages - mean_adv
    dev_ret = returns - mean_ret
    sq_adv, sq_ret = (
        by_axis(jnp.sum(dev_adv * dev_adv), TM_ENV),
        by_axis(jnp.sum(dev_ret * dev_ret), TM_ENV),
    )
    var_adv = sq_adv / samples
    var_ret = sq_ret / samples
    norm_adv = (advantages - mean_adv) / jnp.sqrt(var_adv + 1e-05)
    norm_ret = (returns - mean_ret) / jnp.sqrt(var_ret + 1e-05)
    return (norm_adv, norm_ret)


def shards(rewards, values, last_value, done_steps, horizon_offset, discount_rate, trace_rate):
    steps_dev, envs_dev = rewards.shape
    time_blocks = lax.axis_size(TM)
    position = lax.axis_index(TM)
    horizon = steps_dev * time_blocks // 2
    discount = jnp.exp(-discount_rate)
    retention = discount * jnp.exp(-trace_rate)
    moment_index = position * steps_dev + jnp.arange(steps_dev, dtype=jnp.int32)[:, None]
    ends = [done_steps[:, column][None, :] for column in range(done_steps.shape[1])]
    living, carried = episode_masks(moment_index, ends, horizon_offset[None, :], horizon)
    first_next = from_behind(values[0:1], TM, -1)
    boundary = jnp.where(position == time_blocks - 1, last_value[None, :], first_next)
    next_value = jnp.concatenate([values[1:], boundary], axis=0)
    td_error = rewards + discount[None, :] * living * next_value - values
    decay = retention[None, :] * carried
    partial_value, decayed = suffix_scan(td_error, decay, 0)
    identity = (jnp.zeros_like(partial_value[0]), jnp.ones_like(decayed[0]))
    incoming = prefix((partial_value[0], decayed[0]), TM, compose_blocks, identity)[0]
    advantages = partial_value + decayed * incoming[None, :]
    returns = advantages + values
    norm_adv, norm_ret = statistics(advantages, returns)
    return (
        lax.all_to_all(norm_adv.T, TM, split_axis=0, concat_axis=1, tiled=True),
        lax.all_to_all(norm_ret.T, TM, split_axis=0, concat_axis=1, tiled=True),
    )


def solution(mesh):
    split = Mesh(mesh.devices.reshape(4, 4, 4, 2), ("tm_0", "tm_1", "env_0", "env_1"))
    placed = (P(TM, ENV), P(TM, ENV), P(ENV), P(ENV, None), P(ENV), P(ENV), P(ENV))
    return jax.shard_map(
        shards,
        mesh=split,
        in_specs=placed,
        out_specs=(P(ENV_TM, None), P(ENV_TM, None)),
        check_vma=False,
    )
```

profile of v0, /device:TPU:114, one launch (start us, length us, event | category | flops | bytes accessed | tf_op | source)
XLA Modules:
  0.0 445.4 jit_solution(117539721496437873)
XLA Ops:
  5.2 5.3 %copy.25 = f32[2048,512]{0,1:T(8,128)} copy(f32[2048,512]{1,0:T(8,128)} %param.8) | data formatting | bytes 8388608 | tf_op args[1]
  10.6 5.3 %slice.207 = f32[2047,512]{0,1:T(8,128)} slice(f32[2048,512]{0,1:T(8,128)} %copy.25), slice={[1:2048], [0:512]} | slice | bytes 8384512 | tf_op jit(solution)/shard_map/slice | solution.py:139
  15.9 5.3 %copy.27 = f32[2048,512]{0,1:T(8,128)} copy(f32[2048,512]{1,0:T(8,128)} %param.7) | data formatting | bytes 8388608 | tf_op args[0]
  21.4 6.0 %fusion.3 = f32[2048,512]{0,1:T(8,128)S(1)} fusion(f32[2048,512]{0,1:T(8,128)} %copy.25, f32[2048,512]{0,1:T(8,128)} %copy.27, f32[1,512]{0,1:T(8,128)S(1)} %copy.26, f32[2047,512]{0,1:T(8,128)} %slice.207, f32[512]{0:T(512)S(1)} %get-tuple-element.54, s32[512]{0:T(512)S(1)} %bitcast.34, s32[512]{0:T(512)S(1)} %bitcast.37, s32[512]{0:T(512)S(1)} %bitcast.31, ...), kind=kLoop, calls=%fused_computation.9 | loop fusion | flops 14680064 | bytes 16795648 | tf_op jit(solution)/shard_map/sub | solution.py:140
  28.6 5.3 %multiply_multiply_fusion = (f32[2048,512]{0,1:T(8,128)S(1)}, f32[2048,512]{0,1:T(8,128)S(1)}) fusion(s32[512]{0:T(512)S(1)} %copy-done.18, f32[512]{0:T(512)S(1)} %get-tuple-element.53, s32[2048]{0:T(1024)S(1)} %iota_add_fusion, s32[512]{0:T(512)S(1)} %bitcast.35, s32[512]{0:T(512)S(1)} %bitcast.38, s32[512]{0:T(512)S(1)} %bitcast.32, s32[512]{0:T(512)S(1)} %bitcast.29, ...), kind=kLoop, calls=%fused_computation.35 | loop fusion | flops 29360128 | bytes 16795648 | tf_op jit(solution)/shard_map/mul | solution.py:141
  36.1 5.7 %multiply_add_fusion.10 = (f32[2048,512]{0,1:T(8,128)S(1)}, f32[2048,512]{0,1:T(8,128)S(1)}) fusion(f32[2048,512]{0,1:T(8,128)S(1)} %get-tuple-element.44, f32[2046,512]{0,1:T(8,128)S(1)} %slice.210, f32[2047,512]{0,1:T(8,128)S(1)} %slice.209, s32[512]{0:T(512)S(1)} %copy-done.18, s32[512]{0:T(512)S(1)} %bitcast.36, s32[512]{0:T(512)S(1)} %bitcast.39, ...), kind=kLoop, calls=%fused_computation.32 | loop fusion | flops 30408704 | bytes 20985856 | tf_op jit(solution)/shard_map/add | solution.py:98
  48.3 10.2 %multiply_add_fusion.9 = (f32[2048,512]{0,1:T(8,128)}, f32[2048,512]{0,1:T(8,128)}) fusion(f32[2048,512]{0,1:T(8,128)S(1)} %get-tuple-element.39, f32[2044,512]{0,1:T(8,128)} %slice.212, f32[2048,512]{0,1:T(8,128)} %copy-done, f32[2046,512]{0,1:T(8,128)} %slice.211), kind=kLoop, calls=%fused_computation.30 | loop fusion | flops 3145728 | bytes 25153536 | tf_op jit(solution)/shard_map/add | solution.py:98
  58.5 5.5 %slice.214 = f32[2040,512]{0,1:T(8,128)} slice(f32[2048,512]{0,1:T(8,128)} %get-tuple-element.37), slice={[8:2048], [0:512]} | slice | bytes 8355840 | tf_op jit(solution)/shard_map/slice | solution.py:83
  67.1 10.2 %multiply_add_fusion.8 = (f32[2048,512]{0,1:T(8,128)}, f32[2048,512]{0,1:T(8,128)}) fusion(f32[2048,512]{0,1:T(8,128)S(1)} %copy-done.1, f32[2040,512]{0,1:T(8,128)} %slice.214, f32[2048,512]{0,1:T(8,128)} %get-tuple-element.38, f32[2044,512]{0,1:T(8,128)} %slice.213), kind=kLoop, calls=%fused_computation.28 | loop fusion | flops 3145728 | bytes 25141248 | tf_op jit(solution)/shard_map/add | solution.py:98
  77.3 5.5 %slice.216 = f32[2032,512]{0,1:T(8,128)} slice(f32[2048,512]{0,1:T(8,128)} %get-tuple-element.35), slice={[16:2048], [0:512]} | slice | bytes 8323072 | tf_op jit(solution)/shard_map/slice | solution.py:83
  85.9 10.4 %multiply_add_fusion.7 = (f32[2048,512]{0,1:T(8,128)}, f32[2048,512]{0,1:T(8,128)}) fusion(f32[2048,512]{0,1:T(8,128)S(1)} %copy-done.3, f32[2032,512]{0,1:T(8,128)} %slice.216, f32[2048,512]{0,1:T(8,128)} %get-tuple-element.36, f32[2040,512]{0,1:T(8,128)} %slice.215), kind=kLoop, calls=%fused_computation.26 | loop fusion | flops 3145728 | bytes 25116672 | tf_op jit(solution)/shard_map/add | solution.py:98
  96.3 5.5 %slice.218 = f32[2016,512]{0,1:T(8,128)} slice(f32[2048,512]{0,1:T(8,128)} %get-tuple-element.33), slice={[32:2048], [0:512]} | slice | bytes 8257536 | tf_op jit(solution)/shard_map/slice | solution.py:83
  104.9 10.2 %multiply_add_fusion.6 = (f32[2048,512]{0,1:T(8,128)}, f32[2048,512]{0,1:T(8,128)}) fusion(f32[2048,512]{0,1:T(8,128)S(1)} %copy-done.5, f32[2016,512]{0,1:T(8,128)} %slice.218, f32[2048,512]{0,1:T(8,128)} %get-tuple-element.34, f32[2032,512]{0,1:T(8,128)} %slice.217), kind=kLoop, calls=%fused_computation.24 | loop fusion | flops 3145728 | bytes 25067520 | tf_op jit(solution)/shard_map/add | solution.py:98
  115.0 5.5 %slice.220 = f32[1984,512]{0,1:T(8,128)} slice(f32[2048,512]{0,1:T(8,128)} %get-tuple-element.31), slice={[64:2048], [0:512]} | slice | bytes 8126464 | tf_op jit(solution)/shard_map/slice | solution.py:83
  123.7 10.2 %multiply_add_fusion.5 = (f32[2048,512]{0,1:T(8,128)}, f32[2048,512]{0,1:T(8,128)}) fusion(f32[2048,512]{0,1:T(8,128)S(1)} %copy-done.7, f32[1984,512]{0,1:T(8,128)} %slice.220, f32[2048,512]{0,1:T(8,128)} %get-tuple-element.32, f32[2016,512]{0,1:T(8,128)} %slice.219), kind=kLoop, calls=%fused_computation.22 | loop fusion | flops 3145728 | bytes 24969216 | tf_op jit(solution)/shard_map/add | solution.py:98
  141.4 10.2 %multiply_add_fusion.4 = (f32[2048,512]{0,1:T(8,128)}, f32[2048,512]{0,1:T(8,128)}) fusion(f32[2048,512]{0,1:T(8,128)} %get-tuple-element.29, f32[1920,512]{0,1:T(8,128)} %slice.222, f32[2048,512]{0,1:T(8,128)S(1)} %copy-done.9, f32[1984,512]{0,1:T(8,128)} %slice.221), kind=kLoop, calls=%fused_computation.20 | loop fusion | flops 3145728 | bytes 24772608 | tf_op jit(solution)/shard_map/add | solution.py:98
  156.1 8.3 %multiply_add_fusion.3 = (f32[2048,512]{0,1:T(8,128)}, f32[2048,512]{0,1:T(8,128)}) fusion(f32[2048,512]{0,1:T(8,128)} %get-tuple-element.27, f32[1792,512]{0,1:T(8,128)} %slice.224, f32[2048,512]{0,1:T(8,128)S(1)} %copy-done.10, f32[1920,512]{0,1:T(8,128)S(1)} %slice.223), kind=kLoop, calls=%fused_computation.18 | loop fusion | flops 3145728 | bytes 24379392 | tf_op jit(solution)/shard_map/add | solution.py:98
  171.9 8.0 %multiply_add_fusion.2 = (f32[2048,512]{0,1:T(8,128)}, f32[2048,512]{0,1:T(8,128)}) fusion(f32[2048,512]{0,1:T(8,128)S(1)} %copy-done.12, f32[1536,512]{0,1:T(8,128)} %slice.226, f32[2048,512]{0,1:T(8,128)S(1)} %copy-done.11, f32[1792,512]{0,1:T(8,128)} %slice.225), kind=kLoop, calls=%fused_computation.16 | loop fusion | flops 3145728 | bytes 23592960 | tf_op jit(solution)/shard_map/add | solution.py:98
  186.6 6.7 %multiply_add_fusion.1 = (f32[2048,512]{0,1:T(8,128)S(1)}, f32[2048,512]{0,1:T(8,128)}) fusion(f32[2048,512]{0,1:T(8,128)S(1)} %copy-done.14, f32[1024,512]{0,1:T(8,128)} %slice.228, f32[2048,512]{0,1:T(8,128)S(1)} %copy-done.13, f32[1536,512]{0,1:T(8,128)} %slice.227), kind=kLoop, calls=%fused_computation.14 | loop fusion | flops 3145728 | bytes 22020096 | tf_op jit(solution)/shard_map/add | solution.py:98
  201.9 7.1 %all-to-all-start = ((f32[16,2,512]{2,1,0:T(2,128)}), f32[16,2,512]{2,1,0:T(2,128)S(1)}, u32[]{:S(2)}, u32[]{:S(2)}) async-start(f32[16,2,512]{2,1,0:T(2,128)} %broadcast_in_dim.20), calls=%async_computation | async-start | bytes 131072 | tf_op jit(solution)/shard_map/all_to_all | solution.py:27
  213.8 11.1 %fusion.6 = (f32[]{:T(128)}, f32[2048,512]{0,1:T(8,128)}, f32[2048,512]{0,1:T(8,128)}) fusion(f32[2048,512]{0,1:T(8,128)} %copy.25, f32[2048,512]{0,1:T(8,128)} %copy-done.17, f32[2048,512]{0,1:T(8,128)} %copy-done.16, f32[512]{0:T(512)S(1)} %bitcast.40), kind=kLoop, calls=%fused_computation.55 | loop fusion | flops 4194303 | bytes 20973572 | tf_op jit(solution)/shard_map/reduce_sum | solution.py:111
  228.8 9.1 %all-reduce.27 = (f32[]{:T(128)}, f32[]{:T(128)}) all-reduce(f32[]{:T(128)} %reduce_sum.36, f32[]{:T(128)} %get-tuple-element.18), channel_id=1, replica_groups=mesh['tm_0'=4,'tm_1'=4,'env_0'=4,'env_1'=2] {'tm_0'}, use_global_device_ids=true, to_apply=%region_1.2 | all-reduce | flops 2 | bytes 16 | tf_op jit(solution)/shard_map/psum | solution.py:15
  237.9 9.2 %all-reduce.25 = (f32[]{:T(128)}, f32[]{:T(128)}) all-reduce(f32[]{:T(128)} %get-tuple-element.12, f32[]{:T(128)} %get-tuple-element.13), channel_id=1, replica_groups=mesh['tm_0'=4,'tm_1'=4,'env_0'=4,'env_1'=2] {'tm_1'}, use_global_device_ids=true, to_apply=%region_2.3 | all-reduce | flops 2 | bytes 16 | tf_op jit(solution)/shard_map/psum | solution.py:15
  247.1 9.2 %all-reduce.23 = (f32[]{:T(128)}, f32[]{:T(128)}) all-reduce(f32[]{:T(128)} %get-tuple-element.8, f32[]{:T(128)} %get-tuple-element.9), channel_id=1, replica_groups=mesh['tm_0'=4,'tm_1'=4,'env_0'=4,'env_1'=2] {'env_0'}, use_global_device_ids=true, to_apply=%region_3.4 | all-reduce | flops 2 | bytes 16 | tf_op jit(solution)/shard_map/psum | solution.py:15
  261.1 5.2 %multiply_reduce_fusion = (f32[]{:T(128)}, f32[]{:T(128)}) fusion(f32[2048,512]{0,1:T(8,128)} %get-tuple-element.19, f32[]{:T(128)S(6)} %div.28, f32[2048,512]{0,1:T(8,128)} %get-tuple-element.20, f32[]{:T(128)S(6)} %div.24), kind=kLoop, calls=%fused_computation.10 | loop fusion | flops 6291454 | bytes 8388624 | tf_op jit(solution)/shard_map/reduce_sum | solution.py:118
  266.2 9.3 %all-reduce.26 = (f32[]{:T(128)}, f32[]{:T(128)}) all-reduce(f32[]{:T(128)} %get-tuple-element.58, f32[]{:T(128)} %get-tuple-element.57), channel_id=1, replica_groups=mesh['tm_0'=4,'tm_1'=4,'env_0'=4,'env_1'=2] {'tm_0'}, use_global_device_ids=true, to_apply=%region_6.7 | all-reduce | flops 2 | bytes 16 | tf_op jit(solution)/shard_map/psum | solution.py:15
  275.5 9.6 %all-reduce.24 = (f32[]{:T(128)}, f32[]{:T(128)}) all-reduce(f32[]{:T(128)} %get-tuple-element.10, f32[]{:T(128)} %get-tuple-element.11), channel_id=1, replica_groups=mesh['tm_0'=4,'tm_1'=4,'env_0'=4,'env_1'=2] {'tm_1'}, use_global_device_ids=true, to_apply=%region_7.8 | all-reduce | flops 2 | bytes 16 | tf_op jit(solution)/shard_map/psum | solution.py:15
  285.1 10.8 %all-reduce.22 = (f32[]{:T(128)}, f32[]{:T(128)}) all-reduce(f32[]{:T(128)} %get-tuple-element.6, f32[]{:T(128)} %get-tuple-element.7), channel_id=1, replica_groups=mesh['tm_0'=4,'tm_1'=4,'env_0'=4,'env_1'=2] {'env_0'}, use_global_device_ids=true, to_apply=%region_8.9 | all-reduce | flops 2 | bytes 16 | tf_op jit(solution)/shard_map/psum | solution.py:15
  304.6 8.4 %all-to-all-start.1 = ((f32[16,32,2048]{2,1,0:T(8,128)}), f32[16,32,2048]{2,1,0:T(8,128)}, u32[]{:S(2)}, u32[]{:S(2)}) async-start(f32[16,32,2048]{2,1,0:T(8,128)} %bitcast.24), calls=%async_computation.1 | async-start | bytes 8388608 | tf_op jit(solution)/shard_map/all_to_all | solution.py:149
  318.7 56.0 %all-to-all-done.1 = f32[16,32,2048]{2,1,0:T(8,128)} async-done(((f32[16,32,2048]{2,1,0:T(8,128)}), f32[16,32,2048]{2,1,0:T(8,128)}, u32[]{:S(2)}, u32[]{:S(2)}) %all-to-all-start.1) | async-done | bytes 4194336 | tf_op jit(solution)/shard_map/all_to_all | solution.py:149
  374.7 6.9 %all-to-all-start.2 = ((f32[16,32,2048]{2,1,0:T(8,128)}), f32[16,32,2048]{2,1,0:T(8,128)}, u32[]{:S(2)}, u32[]{:S(2)}) async-start(f32[16,32,2048]{2,1,0:T(8,128)} %bitcast.25), calls=%async_computation.2 | async-start | bytes 8388608 | tf_op jit(solution)/shard_map/all_to_all | solution.py:150
  386.4 54.2 %all-to-all-done.2 = f32[16,32,2048]{2,1,0:T(8,128)} async-done(((f32[16,32,2048]{2,1,0:T(8,128)}), f32[16,32,2048]{2,1,0:T(8,128)}, u32[]{:S(2)}, u32[]{:S(2)}) %all-to-all-start.2) | async-done | bytes 4194336 | tf_op jit(solution)/shard_map/all_to_all | solution.py:150
  (104 shorter events, 96.3 us)
Async XLA Ops:
  1.4 19.9 %collective-permute-start = (f32[1,512]{1,0:T(1,128)S(1)}, f32[1,512]{1,0:T(1,128)S(1)}, u32[]{:S(2)}, u32[]{:S(2)}) collective-permute-start(f32[1,512]{1,0:T(1,128)S(1)} %slice.161), channel_id=1, source_target_pairs={{8,0},{16,8},{24,16},{32,24},{40,32},{48,40},{56,48},{64,56},{72,6... | collective-permute-start | bytes 6152 | tf_op jit(solution)/shard_map/ppermute | solution.py:22
  15.9 5.4 %copy-start.19 = (f32[512]{0:T(512)S(1)}, f32[512]{0:T(512)}, u32[]{:S(2)}) copy-start(f32[512]{0:T(512)} %param.9) | copy-start | bytes 6148
  27.4 1.2 copy-start.18
  41.8 3.4 copy-start
  58.5 5.5 %copy-start.2 = (f32[2048,512]{0,1:T(8,128)S(1)}, f32[2048,512]{0,1:T(8,128)}, u32[]{:S(2)}) copy-start(f32[2048,512]{0,1:T(8,128)} %get-tuple-element.38) | copy-start | bytes 12582916
  64.0 3.1 copy-start.1
  77.3 5.5 %copy-start.4 = (f32[2048,512]{0,1:T(8,128)S(1)}, f32[2048,512]{0,1:T(8,128)}, u32[]{:S(2)}) copy-start(f32[2048,512]{0,1:T(8,128)} %get-tuple-element.36) | copy-start | bytes 12582916
  82.8 3.1 copy-start.3
  96.3 5.5 %copy-start.6 = (f32[2048,512]{0,1:T(8,128)S(1)}, f32[2048,512]{0,1:T(8,128)}, u32[]{:S(2)}) copy-start(f32[2048,512]{0,1:T(8,128)} %get-tuple-element.34) | copy-start | bytes 12582916
  101.8 3.1 copy-start.5
  115.0 5.5 %copy-start.8 = (f32[2048,512]{0,1:T(8,128)S(1)}, f32[2048,512]{0,1:T(8,128)}, u32[]{:S(2)}) copy-start(f32[2048,512]{0,1:T(8,128)} %get-tuple-element.32) | copy-start | bytes 12582916
  120.5 3.1 copy-start.7
  133.8 4.4 copy-start.9
  151.5 4.2 copy-start.10
  164.4 4.0 copy-start.11
  168.4 3.5 copy-start.12
  179.9 3.4 copy-start.13
  183.3 3.3 copy-start.14
  193.3 2.0 copy-start.17
  195.4 2.8 copy-start.15
  199.1 2.0 copy-start.16
  201.9 11.1 %all-to-all-start = ((f32[16,2,512]{2,1,0:T(2,128)}), f32[16,2,512]{2,1,0:T(2,128)S(1)}, u32[]{:S(2)}, u32[]{:S(2)}) async-start(f32[16,2,512]{2,1,0:T(2,128)} %broadcast_in_dim.20), calls=%async_computation | async-start | bytes 131072 | tf_op jit(solution)/shard_map/all_to_all | solution.py:27
  304.6 70.1 %all-to-all-start.1 = ((f32[16,32,2048]{2,1,0:T(8,128)}), f32[16,32,2048]{2,1,0:T(8,128)}, u32[]{:S(2)}, u32[]{:S(2)}) async-start(f32[16,32,2048]{2,1,0:T(8,128)} %bitcast.24), calls=%async_computation.1 | async-start | bytes 8388608 | tf_op jit(solution)/shard_map/all_to_all | solution.py:149
  374.7 65.8 %all-to-all-start.2 = ((f32[16,32,2048]{2,1,0:T(8,128)}), f32[16,32,2048]{2,1,0:T(8,128)}, u32[]{:S(2)}, u32[]{:S(2)}) async-start(f32[16,32,2048]{2,1,0:T(8,128)} %bitcast.25), calls=%async_computation.2 | async-start | bytes 8388608 | tf_op jit(solution)/shard_map/all_to_all | solution.py:150
where the time goes:
time: 453 us; the launch traced here: 445 us
  other arithmetic  133 us (29%)
  waiting for transfers between devices  114 us (25%)
  local copies, waits for them, and re-layouts  106 us (23%)
  blocking collectives  63.7 us (14%)
  starting transfers between devices  24.8 us (5%)
    add x10, other arithmetic, suffix_scan(): partial_value = partial_value + decayed * later_partial  89.9 us
    slice x22, local copies, waits for them, and re-layouts, shift_later(): kept = lax.slice_in_dim(field, distance, length, 1, axis)  69.8 us
    psum x8, blocking collectives, by_axis(): value = lax.psum(value, axis)  63.7 us
    all_to_all x1, waiting for transfers between devices, shards(): lax.all_to_all(norm_adv.T, TM, split_axis=0, concat_axis=1, tiled=True)  56 us
    all_to_all x1, waiting for transfers between devices, shards(): lax.all_to_all(norm_ret.T, TM, split_axis=0, concat_axis=1, tiled=True)  54.2 us
    unnamed x42, local copies, waits for them, and re-layouts  18.3 us
    reduce_sum x1, other arithmetic, statistics(): jnp.sum(returns)  11.1 us
  transfers between devices with their start and end apart: 4, of which 3 were waited for; matrix products, arithmetic and copies ran while one was open for 6% of the time, Pallas kernels for 0%

commit v1 on v0

--- a/solution.py
+++ b/solution.py
@@ -12,7 +12,8 @@
 
 def by_axis(value, axes):
     for axis in axes:
-        value = lax.psum(value, axis)
+        words_lift = lambda in_array, a_name: lax.all_gather(in_array, a_name).sum(axis=0)
+        value = words_lift(value, a_name=axis)
     return value
 
 

time: 453 us -> 481 us (1.062)
  local copies, waits for them, and re-layouts: 106 us -> 129 us
  other arithmetic: 133 us -> 143 us
  blocking collectives: 63.7 us -> 58.1 us
    psum x8 -> x0, blocking collectives: 63.7 us -> none  [by_axis(): value = lax.psum(value, axis)]
    unnamed x0 -> x8, blocking collectives: none -> 58.1 us
    unnamed x42 -> x78, local copies, waits for them, and re-layouts: 18.3 us -> 41.5 us
    reduce_sum x0 -> x16, other arithmetic: none -> 10.5 us  [by_axis(): lax.all_gather(in_array, a_name).sum(axis=0)]
where the time goes in v1:
time: 481 us; the launch traced here: 473 us
  other arithmetic  143 us (30%)
  local copies, waits for them, and re-layouts  129 us (27%)
  waiting for transfers between devices  114 us (24%)
  blocking collectives  58.1 us (12%)
  starting transfers between devices  24.7 us (5%)
    add x10, other arithmetic, suffix_scan(): partial_value = partial_value + decayed * later_partial  90 us
    slice x22, local copies, waits for them, and re-layouts, shift_later(): kept = lax.slice_in_dim(field, distance, length, 1, axis)  68.8 us
    unnamed x8, blocking collectives  58.1 us
    all_to_all x1, waiting for transfers between devices, shards(): lax.all_to_all(norm_ret.T, TM, split_axis=0, concat_axis=1, tiled=True)  55.4 us
    all_to_all x1, waiting for transfers between devices, shards(): lax.all_to_all(norm_adv.T, TM, split_axis=0, concat_axis=1, tiled=True)  54.2 us
    unnamed x78, local copies, waits for them, and re-layouts  41.5 us
    reduce_sum x1, other arithmetic, statistics(): jnp.sum(returns)  11.1 us
    reduce_sum x16, other arithmetic, by_axis(): lax.all_gather(in_array, a_name).sum(axis=0)  10.5 us
  transfers between devices with their start and end apart: 4, of which 3 were waited for; matrix products, arithmetic and copies ran while one was open for 6% of the time, Pallas kernels for 0%

profile of v1, /device:TPU:114, one launch (start us, length us, event | category | flops | bytes accessed | tf_op | source)
XLA Modules:
  0.0 472.8 jit_solution(8164486393100877218)
XLA Ops:
  5.2 5.3 %copy.25 = f32[2048,512]{0,1:T(8,128)} copy(f32[2048,512]{1,0:T(8,128)} %param.8) | data formatting | bytes 8388608 | tf_op args[1]
  10.6 5.3 %slice.207 = f32[2047,512]{0,1:T(8,128)} slice(f32[2048,512]{0,1:T(8,128)} %copy.25), slice={[1:2048], [0:512]} | slice | bytes 8384512 | tf_op jit(solution)/shard_map/slice | solution.py:140
  15.9 5.4 %copy.27 = f32[2048,512]{0,1:T(8,128)} copy(f32[2048,512]{1,0:T(8,128)} %param.7) | data formatting | bytes 8388608 | tf_op args[0]
  22.0 6.0 %fusion.3 = f32[2048,512]{0,1:T(8,128)S(1)} fusion(f32[2048,512]{0,1:T(8,128)} %copy.25, f32[2048,512]{0,1:T(8,128)} %copy.27, f32[1,512]{0,1:T(8,128)S(1)} %copy.26, f32[2047,512]{0,1:T(8,128)} %slice.207, f32[512]{0:T(512)S(1)} %get-tuple-element.54, s32[512]{0:T(512)S(1)} %bitcast.54, s32[512]{0:T(512)S(1)} %bitcast.57, s32[512]{0:T(512)S(1)} %bitcast.51, ...), kind=kLoop, calls=%fused_computation.9 | loop fusion | flops 14680064 | bytes 16795648 | tf_op jit(solution)/shard_map/sub | solution.py:141
  29.2 5.3 %multiply_multiply_fusion = (f32[2048,512]{0,1:T(8,128)S(1)}, f32[2048,512]{0,1:T(8,128)S(1)}) fusion(s32[512]{0:T(512)S(1)} %copy-done.14, f32[512]{0:T(512)S(1)} %get-tuple-element.53, s32[2048]{0:T(1024)S(1)} %iota_add_fusion, s32[512]{0:T(512)S(1)} %bitcast.55, s32[512]{0:T(512)S(1)} %bitcast.58, s32[512]{0:T(512)S(1)} %bitcast.52, s32[512]{0:T(512)S(1)} %bitcast.49, ...), kind=kLoop, calls=%fused_computation.35 | loop fusion | flops 29360128 | bytes 16795648 | tf_op jit(solution)/shard_map/mul | solution.py:142
  36.7 5.7 %multiply_add_fusion.10 = (f32[2048,512]{0,1:T(8,128)S(1)}, f32[2048,512]{0,1:T(8,128)S(1)}) fusion(f32[2048,512]{0,1:T(8,128)S(1)} %get-tuple-element.44, f32[2046,512]{0,1:T(8,128)S(1)} %slice.210, f32[2047,512]{0,1:T(8,128)S(1)} %slice.209, s32[512]{0:T(512)S(1)} %copy-done.14, s32[512]{0:T(512)S(1)} %bitcast.56, s32[512]{0:T(512)S(1)} %bitcast.59, ...), kind=kLoop, calls=%fused_computation.32 | loop fusion | flops 30408704 | bytes 20985856 | tf_op jit(solution)/shard_map/add | solution.py:99
  48.8 10.2 %multiply_add_fusion.9 = (f32[2048,512]{0,1:T(8,128)}, f32[2048,512]{0,1:T(8,128)}) fusion(f32[2048,512]{0,1:T(8,128)S(1)} %get-tuple-element.39, f32[2044,512]{0,1:T(8,128)} %slice.212, f32[2048,512]{0,1:T(8,128)} %copy-done, f32[2046,512]{0,1:T(8,128)} %slice.211), kind=kLoop, calls=%fused_computation.30 | loop fusion | flops 3145728 | bytes 25153536 | tf_op jit(solution)/shard_map/add | solution.py:99
  59.0 5.5 %slice.213 = f32[2044,512]{0,1:T(8,128)} slice(f32[2048,512]{0,1:T(8,128)} %get-tuple-element.38), slice={[4:2048], [0:512]} | slice | bytes 8372224 | tf_op jit(solution)/shard_map/slice | solution.py:84
  67.6 10.2 %multiply_add_fusion.8 = (f32[2048,512]{0,1:T(8,128)}, f32[2048,512]{0,1:T(8,128)}) fusion(f32[2048,512]{0,1:T(8,128)S(1)} %copy-done.1, f32[2040,512]{0,1:T(8,128)} %slice.214, f32[2048,512]{0,1:T(8,128)} %get-tuple-element.38, f32[2044,512]{0,1:T(8,128)} %slice.213), kind=kLoop, calls=%fused_computation.28 | loop fusion | flops 3145728 | bytes 25141248 | tf_op jit(solution)/shard_map/add | solution.py:99
  77.8 5.5 %slice.215 = f32[2040,512]{0,1:T(8,128)} slice(f32[2048,512]{0,1:T(8,128)} %get-tuple-element.36), slice={[8:2048], [0:512]} | slice | bytes 8355840 | tf_op jit(solution)/shard_map/slice | solution.py:84
  86.5 10.6 %multiply_add_fusion.7 = (f32[2048,512]{0,1:T(8,128)}, f32[2048,512]{0,1:T(8,128)}) fusion(f32[2048,512]{0,1:T(8,128)S(1)} %copy-done.2, f32[2032,512]{0,1:T(8,128)} %slice.216, f32[2048,512]{0,1:T(8,128)} %get-tuple-element.36, f32[2040,512]{0,1:T(8,128)} %slice.215), kind=kLoop, calls=%fused_computation.26 | loop fusion | flops 3145728 | bytes 25116672 | tf_op jit(solution)/shard_map/add | solution.py:99
  97.0 5.5 %slice.217 = f32[2032,512]{0,1:T(8,128)} slice(f32[2048,512]{0,1:T(8,128)} %get-tuple-element.34), slice={[16:2048], [0:512]} | slice | bytes 8323072 | tf_op jit(solution)/shard_map/slice | solution.py:84
  105.7 10.2 %multiply_add_fusion.6 = (f32[2048,512]{0,1:T(8,128)}, f32[2048,512]{0,1:T(8,128)}) fusion(f32[2048,512]{0,1:T(8,128)S(1)} %copy-done.3, f32[2016,512]{0,1:T(8,128)} %slice.218, f32[2048,512]{0,1:T(8,128)} %get-tuple-element.34, f32[2032,512]{0,1:T(8,128)} %slice.217), kind=kLoop, calls=%fused_computation.24 | loop fusion | flops 3145728 | bytes 25067520 | tf_op jit(solution)/shard_map/add | solution.py:99
  115.9 5.5 %slice.219 = f32[2016,512]{0,1:T(8,128)} slice(f32[2048,512]{0,1:T(8,128)} %get-tuple-element.32), slice={[32:2048], [0:512]} | slice | bytes 8257536 | tf_op jit(solution)/shard_map/slice | solution.py:84
  124.5 10.2 %multiply_add_fusion.5 = (f32[2048,512]{0,1:T(8,128)}, f32[2048,512]{0,1:T(8,128)}) fusion(f32[2048,512]{0,1:T(8,128)S(1)} %copy-done.4, f32[1984,512]{0,1:T(8,128)} %slice.220, f32[2048,512]{0,1:T(8,128)} %get-tuple-element.32, f32[2016,512]{0,1:T(8,128)} %slice.219), kind=kLoop, calls=%fused_computation.22 | loop fusion | flops 3145728 | bytes 24969216 | tf_op jit(solution)/shard_map/add | solution.py:99
  134.7 5.5 %slice.221 = f32[1984,512]{0,1:T(8,128)} slice(f32[2048,512]{0,1:T(8,128)} %get-tuple-element.30), slice={[64:2048], [0:512]} | slice | bytes 8126464 | tf_op jit(solution)/shard_map/slice | solution.py:84
  143.8 9.9 %multiply_add_fusion.4 = (f32[2048,512]{0,1:T(8,128)}, f32[2048,512]{0,1:T(8,128)}) fusion(f32[2048,512]{0,1:T(8,128)} %get-tuple-element.29, f32[1920,512]{0,1:T(8,128)} %slice.222, f32[2048,512]{0,1:T(8,128)S(1)} %copy-done.5, f32[1984,512]{0,1:T(8,128)} %slice.221), kind=kLoop, calls=%fused_computation.20 | loop fusion | flops 3145728 | bytes 24772608 | tf_op jit(solution)/shard_map/add | solution.py:99
  159.1 8.3 %multiply_add_fusion.3 = (f32[2048,512]{0,1:T(8,128)}, f32[2048,512]{0,1:T(8,128)}) fusion(f32[2048,512]{0,1:T(8,128)} %get-tuple-element.27, f32[1792,512]{0,1:T(8,128)} %slice.224, f32[2048,512]{0,1:T(8,128)S(1)} %copy-done.7, f32[1920,512]{0,1:T(8,128)S(1)} %slice.223), kind=kLoop, calls=%fused_computation.18 | loop fusion | flops 3145728 | bytes 24379392 | tf_op jit(solution)/shard_map/add | solution.py:99
  175.0 8.0 %multiply_add_fusion.2 = (f32[2048,512]{0,1:T(8,128)}, f32[2048,512]{0,1:T(8,128)}) fusion(f32[2048,512]{0,1:T(8,128)S(1)} %copy-done.10, f32[1536,512]{0,1:T(8,128)} %slice.226, f32[2048,512]{0,1:T(8,128)S(1)} %copy-done.9, f32[1792,512]{0,1:T(8,128)} %slice.225), kind=kLoop, calls=%fused_computation.16 | loop fusion | flops 3145728 | bytes 23592960 | tf_op jit(solution)/shard_map/add | solution.py:99
  189.3 6.7 %multiply_add_fusion.1 = (f32[2048,512]{0,1:T(8,128)}, f32[2048,512]{0,1:T(8,128)S(1)}) fusion(f32[2048,512]{0,1:T(8,128)S(1)} %copy-done.12, f32[1024,512]{0,1:T(8,128)} %slice.228, f32[2048,512]{0,1:T(8,128)S(1)} %copy-done.11, f32[1536,512]{0,1:T(8,128)} %slice.227), kind=kLoop, calls=%fused_computation.14 | loop fusion | flops 3145728 | bytes 22020096 | tf_op jit(solution)/shard_map/add | solution.py:99
  200.8 7.1 %all-to-all-start = ((f32[16,2,512]{2,1,0:T(2,128)}), f32[16,2,512]{2,1,0:T(2,128)S(1)}, u32[]{:S(2)}, u32[]{:S(2)}) async-start(f32[16,2,512]{2,1,0:T(2,128)} %broadcast_in_dim.20), calls=%async_computation | async-start | bytes 131072 | tf_op jit(solution)/shard_map/all_to_all | solution.py:28
  212.7 11.1 %fusion.6 = (f32[]{:T(128)}, f32[2048,512]{0,1:T(8,128)}, f32[2048,512]{0,1:T(8,128)}) fusion(f32[2048,512]{0,1:T(8,128)} %copy.25, f32[2048,512]{0,1:T(8,128)} %get-tuple-element.21, f32[2048,512]{0,1:T(8,128)} %copy-done.13, f32[512]{0:T(512)S(1)} %bitcast.60), kind=kLoop, calls=%fused_computation.55 | loop fusion | flops 4194303 | bytes 20973572 | tf_op jit(solution)/shard_map/reduce_sum | solution.py:112
  231.1 8.5 %all-reduce.43 = (f32[4]{0:T(128)S(1)}, f32[4]{0:T(128)S(1)}) all-reduce(f32[4]{0:T(128)S(1)} %dynamic-update-slice, f32[4]{0:T(128)S(1)} %dynamic-update-slice.8), channel_id=1, replica_groups=mesh['tm_0'=4,'tm_1'=4,'env_0'=4,'env_1'=2] {'tm_0'}, use_global_device_ids=true, to_apply=%add.22 | all-reduce | flops 8 | bytes 64
  244.2 8.5 %all-reduce.41 = (f32[4]{0:T(128)S(1)}, f32[4]{0:T(128)S(1)}) all-reduce(f32[4]{0:T(128)S(1)} %dynamic-update-slice.1, f32[4]{0:T(128)S(1)} %dynamic-update-slice.9), channel_id=1, replica_groups=mesh['tm_0'=4,'tm_1'=4,'env_0'=4,'env_1'=2] {'tm_1'}, use_global_device_ids=true, to_apply=%add.23 | all-reduce | flops 8 | bytes 64
  257.2 8.6 %all-reduce.39 = (f32[4]{0:T(128)S(1)}, f32[4]{0:T(128)S(1)}) all-reduce(f32[4]{0:T(128)S(1)} %dynamic-update-slice.2, f32[4]{0:T(128)S(1)} %dynamic-update-slice.10), channel_id=1, replica_groups=mesh['tm_0'=4,'tm_1'=4,'env_0'=4,'env_1'=2] {'env_0'}, use_global_device_ids=true, to_apply=%add.24 | all-reduce | flops 8 | bytes 64
  283.0 8.6 %all-reduce.42 = (f32[4]{0:T(128)S(1)}, f32[4]{0:T(128)S(1)}) all-reduce(f32[4]{0:T(128)S(1)} %dynamic-update-slice.4, f32[4]{0:T(128)S(1)} %dynamic-update-slice.12), channel_id=1, replica_groups=mesh['tm_0'=4,'tm_1'=4,'env_0'=4,'env_1'=2] {'tm_0'}, use_global_device_ids=true, to_apply=%add.26 | all-reduce | flops 8 | bytes 64
  295.8 9.0 %all-reduce.40 = (f32[4]{0:T(128)S(1)}, f32[4]{0:T(128)S(1)}) all-reduce(f32[4]{0:T(128)S(1)} %dynamic-update-slice.5, f32[4]{0:T(128)S(1)} %dynamic-update-slice.13), channel_id=1, replica_groups=mesh['tm_0'=4,'tm_1'=4,'env_0'=4,'env_1'=2] {'tm_1'}, use_global_device_ids=true, to_apply=%add.27 | all-reduce | flops 8 | bytes 64
  308.8 10.1 %all-reduce.38 = (f32[4]{0:T(128)S(1)}, f32[4]{0:T(128)S(1)}) all-reduce(f32[4]{0:T(128)S(1)} %dynamic-update-slice.6, f32[4]{0:T(128)S(1)} %dynamic-update-slice.14), channel_id=1, replica_groups=mesh['tm_0'=4,'tm_1'=4,'env_0'=4,'env_1'=2] {'env_0'}, use_global_device_ids=true, to_apply=%add.28 | all-reduce | flops 8 | bytes 64
  332.0 8.4 %all-to-all-start.2 = ((f32[16,32,2048]{2,1,0:T(8,128)}), f32[16,32,2048]{2,1,0:T(8,128)}, u32[]{:S(2)}, u32[]{:S(2)}) async-start(f32[16,32,2048]{2,1,0:T(8,128)} %bitcast.44), calls=%async_computation.2 | async-start | bytes 8388608 | tf_op jit(solution)/shard_map/all_to_all | solution.py:151
  346.7 55.4 %all-to-all-done.2 = f32[16,32,2048]{2,1,0:T(8,128)} async-done(((f32[16,32,2048]{2,1,0:T(8,128)}), f32[16,32,2048]{2,1,0:T(8,128)}, u32[]{:S(2)}, u32[]{:S(2)}) %all-to-all-start.2) | async-done | bytes 4194336 | tf_op jit(solution)/shard_map/all_to_all | solution.py:151
  402.1 6.9 %all-to-all-start.1 = ((f32[16,32,2048]{2,1,0:T(8,128)}), f32[16,32,2048]{2,1,0:T(8,128)}, u32[]{:S(2)}, u32[]{:S(2)}) async-start(f32[16,32,2048]{2,1,0:T(8,128)} %bitcast.45), calls=%async_computation.1 | async-start | bytes 8388608 | tf_op jit(solution)/shard_map/all_to_all | solution.py:150
  413.7 54.2 %all-to-all-done.1 = f32[16,32,2048]{2,1,0:T(8,128)} async-done(((f32[16,32,2048]{2,1,0:T(8,128)}), f32[16,32,2048]{2,1,0:T(8,128)}, u32[]{:S(2)}, u32[]{:S(2)}) %all-to-all-start.1) | async-done | bytes 4194336 | tf_op jit(solution)/shard_map/all_to_all | solution.py:150
  (156 shorter events, 128.2 us)
Async XLA Ops:
  1.4 20.5 %collective-permute-start = (f32[1,512]{1,0:T(1,128)S(1)}, f32[1,512]{1,0:T(1,128)S(1)}, u32[]{:S(2)}, u32[]{:S(2)}) collective-permute-start(f32[1,512]{1,0:T(1,128)S(1)} %slice.161), channel_id=1, source_target_pairs={{8,0},{16,8},{24,16},{32,24},{40,32},{48,40},{56,48},{64,56},{72,6... | collective-permute-start | bytes 6152 | tf_op jit(solution)/shard_map/ppermute | solution.py:23
  15.8 5.4 %copy-start.19 = (u32[128]{0:T(128)S(1)}, u32[128]{0:T(128)}, u32[]{:S(2)}) copy-start(u32[128]{0:T(128)} %constant.114) | copy-start | bytes 1540
  15.9 6.0 %copy-start.15 = (f32[512]{0:T(512)S(1)}, f32[512]{0:T(512)}, u32[]{:S(2)}) copy-start(f32[512]{0:T(512)} %param.9) | copy-start | bytes 6148
  28.0 1.2 copy-start.14
  42.4 3.2 copy-start
  59.0 5.5 %copy-start.1 = (f32[2048,512]{0,1:T(8,128)S(1)}, f32[2048,512]{0,1:T(8,128)}, u32[]{:S(2)}) copy-start(f32[2048,512]{0,1:T(8,128)} %get-tuple-element.37) | copy-start | bytes 12582916
  77.8 5.5 %copy-start.2 = (f32[2048,512]{0,1:T(8,128)S(1)}, f32[2048,512]{0,1:T(8,128)}, u32[]{:S(2)}) copy-start(f32[2048,512]{0,1:T(8,128)} %get-tuple-element.35) | copy-start | bytes 12582916
  97.0 5.5 %copy-start.3 = (f32[2048,512]{0,1:T(8,128)S(1)}, f32[2048,512]{0,1:T(8,128)}, u32[]{:S(2)}) copy-start(f32[2048,512]{0,1:T(8,128)} %get-tuple-element.33) | copy-start | bytes 12582916
  115.9 5.5 %copy-start.4 = (f32[2048,512]{0,1:T(8,128)S(1)}, f32[2048,512]{0,1:T(8,128)}, u32[]{:S(2)}) copy-start(f32[2048,512]{0,1:T(8,128)} %get-tuple-element.31) | copy-start | bytes 12582916
  134.7 5.5 %copy-start.6 = (f32[2048,512]{0,1:T(8,128)S(1)}, f32[2048,512]{0,1:T(8,128)}, u32[]{:S(2)}) copy-start(f32[2048,512]{0,1:T(8,128)} %get-tuple-element.29) | copy-start | bytes 12582916
  140.2 3.6 copy-start.5
  153.7 3.4 copy-start.8
  156.2 2.9 copy-start.7
  167.4 4.3 copy-start.10
  171.7 3.3 copy-start.9
  183.0 3.9 copy-start.12
  183.0 6.3 %copy-start.11 = (f32[2048,512]{0,1:T(8,128)S(1)}, f32[2048,512]{0,1:T(8,128)}, u32[]{:S(2)}) copy-start(f32[2048,512]{0,1:T(8,128)} %get-tuple-element.24) | copy-start | bytes 12582916
  196.9 1.9 copy-start.13
  200.8 11.1 %all-to-all-start = ((f32[16,2,512]{2,1,0:T(2,128)}), f32[16,2,512]{2,1,0:T(2,128)S(1)}, u32[]{:S(2)}, u32[]{:S(2)}) async-start(f32[16,2,512]{2,1,0:T(2,128)} %broadcast_in_dim.20), calls=%async_computation | async-start | bytes 131072 | tf_op jit(solution)/shard_map/all_to_all | solution.py:28
  223.7 6.7 %copy-start.18 = (u32[128]{0:T(128)S(1)}, u32[128]{0:T(128)}, u32[]{:S(2)}) copy-start(u32[128]{0:T(128)} %constant.119) | copy-start | bytes 1540
  223.7 19.9 %copy-start.17 = (u32[128]{0:T(128)S(1)}, u32[128]{0:T(128)}, u32[]{:S(2)}) copy-start(u32[128]{0:T(128)} %constant.124) | copy-start | bytes 1540
  223.7 32.9 %copy-start.16 = (u32[128]{0:T(128)S(1)}, u32[128]{0:T(128)}, u32[]{:S(2)}) copy-start(u32[128]{0:T(128)} %constant.129) | copy-start | bytes 1540
  332.0 70.1 %all-to-all-start.2 = ((f32[16,32,2048]{2,1,0:T(8,128)}), f32[16,32,2048]{2,1,0:T(8,128)}, u32[]{:S(2)}, u32[]{:S(2)}) async-start(f32[16,32,2048]{2,1,0:T(8,128)} %bitcast.44), calls=%async_computation.2 | async-start | bytes 8388608 | tf_op jit(solution)/shard_map/all_to_all | solution.py:151
  402.1 65.8 %all-to-all-start.1 = ((f32[16,32,2048]{2,1,0:T(8,128)}), f32[16,32,2048]{2,1,0:T(8,128)}, u32[]{:S(2)}, u32[]{:S(2)}) async-start(f32[16,32,2048]{2,1,0:T(8,128)} %bitcast.45), calls=%async_computation.1 | async-start | bytes 8388608 | tf_op jit(solution)/shard_map/all_to_all | solution.py:150
